TPU v7x, 32 devices: a whole 2x2x4 slice. The times are simulated.
32 devices in a mesh: tm: 2 (over core), height: 16 (over z, y, x).
Axes of the slice: x: 2, y: 2, z: 4, core: 2. Of those that a mesh axis runs over, the one named last changes fastest.
Arguments:
- clip: bfloat16 [4, 128, 48, 256], P('tm', 'height'), may hold values from -6 to 6
- teacher: bfloat16 [4, 128, 48, 256], P('tm', 'height'), may hold values from -6 to 6
- kernel_one: bfloat16 [6912, 256], P('height'), may hold values from -0.078125 to 0.078125
- kernel_two: bfloat16 [6912, 256], P('height'), may hold values from -0.078125 to 0.078125
Outputs:
- student: bfloat16 [4, 128, 48, 256], P('tm', 'height')
- grad_one: float32 [6912, 256], P('height')
- grad_two: float32 [6912, 256], P('height')
All inputs are finite; a program needn't handle non-finite values.
Results may differ from a plain program's by a relative error of at most 0.013.
Values may be sent and summed in bfloat16 or wider, within the bound.
No kernel may reach another device: no remote copies, remote signals or barrier semaphores. Data moves between devices by JAX's collectives and lax.ppermute only.
A program may use at most 128 MiB of HBM per device.

v0:
```python
import math
import jax
import jax.numpy as jnp
from jax import lax
from jax.sharding import PartitionSpec as P


def shifted(value, axis, by):
    count = lax.axis_size(axis)
    pairs = [(i, i + by) for i in range(count) if 0 <= i + by < count]
    return lax.ppermute(value, axis, pairs)


def extended_2(cells, sides, width):
    for axis, dim in sides:
        count = lax.axis_size(axis)
        ends = count - 1
        head = lax.slice_in_dim(cells, 0, width, axis=dim)
        tail = lax.slice_in_dim(cells, cells.shape[dim] - width, cells.shape[dim], axis=dim)
        cells = jnp.concatenate(
            [
                lax.ppermute(tail, axis, [(i, (i + 1) % count) for i in range(ends)]),
                cells,
                lax.ppermute(head, axis, [((i + 1) % count, i) for i in range(ends)]),
            ],
            axis=dim,
        )
    return cells


def tap_offsets():
    return [(t_off, h_off, w_off) for t_off in range(3) for h_off in range(3) for w_off in range(3)]


def widen(stacked):
    return jnp.pad(stacked, ((0, 0), (0, 0), (1, 1), (0, 0)))


def clip_edges(rimmed):
    place = lax.axis_index("height")
    blocks = lax.axis_size("height")
    rows_n = rimmed.shape[1]
    row_ids = jnp.arange(rows_n, dtype=jnp.int32)
    cut = jnp.logical_or(
        jnp.logical_and(row_ids == 0, place == 0),
        jnp.logical_and(row_ids == rows_n - 1, place == blocks - 1),
    )
    return jnp.where(cut[None, :, None, None], jnp.zeros_like(rimmed), rimmed)


def causal_patches(values):
    frames_n, height_n, width_n, chans = values.shape
    earlier = shifted(values, "tm", 1)
    extended = jnp.concatenate([earlier, values], axis=0)
    rimmed = clip_edges(extended_2(extended, (("height", 1),), 1))
    padded = widen(rimmed)
    pieces = [
        padded[t_off : t_off + frames_n, h_off : h_off + height_n, w_off : w_off + width_n]
        for t_off, h_off, w_off in tap_offsets()
    ]
    return jnp.stack(pieces, axis=3).reshape(frames_n * height_n * width_n, 27 * chans)


def future_patches(grads):
    frames_n, height_n, width_n, chans = grads.shape
    later = shifted(grads, "tm", -1)
    extended = jnp.concatenate([grads, later], axis=0)
    rimmed = clip_edges(extended_2(extended, (("height", 1),), 1))
    padded = widen(rimmed)
    pieces = [
        padded[
            2 - t_off : 2 - t_off + frames_n,
            2 - h_off : 2 - h_off + height_n,
            2 - w_off : 2 - w_off + width_n,
        ]
        for t_off, h_off, w_off in tap_offsets()
    ]
    return jnp.stack(pieces, axis=3).reshape(frames_n * height_n * width_n, 27, chans)


def reduce_grad(local_grad):
    owned = lax.psum_scatter(
        local_grad.astype(jnp.bfloat16), "height", scatter_dimension=0, tiled=True
    )
    return lax.psum(owned, "tm").astype(jnp.float32)


def shards(clip, teacher, kernel_one, kernel_two):
    frames_n, height_n, width_n, chans = clip.shape
    full_one = lax.all_gather(kernel_one, "height", axis=0, tiled=True)
    patches_clip = causal_patches(clip)
    pre_act = jnp.dot(patches_clip, full_one, preferred_element_type=jnp.float32)
    hidden = jax.nn.silu(pre_act).astype(jnp.bfloat16)
    full_two = lax.all_gather(kernel_two, "height", axis=0, tiled=True)
    patches_hidden = causal_patches(hidden.reshape(frames_n, height_n, width_n, chans))
    branch = jnp.dot(patches_hidden, full_two, preferred_element_type=jnp.float32)
    output = clip.reshape(-1, chans).astype(jnp.float32) + branch
    count_all = frames_n * lax.axis_size("tm") * height_n * lax.axis_size("height") * width_n
    factor = 1.0 / math.sqrt(count_all)
    grad_out = ((output - teacher.reshape(-1, chans).astype(jnp.float32)) * factor).astype(
        jnp.bfloat16
    )
    contract_rows = (((0,), (0,)), ((), ()))
    grad_two = reduce_grad(
        lax.dot_general(patches_hidden, grad_out, contract_rows, preferred_element_type=jnp.float32)
    )
    grad_patches = future_patches(grad_out.reshape(frames_n, height_n, width_n, chans))
    grad_hidden = jnp.einsum(
        "rkc,kdc->rd",
        grad_patches,
        full_two.reshape(27, chans, chans),
        preferred_element_type=jnp.float32,
    )
    sigmoid_pre = jax.nn.sigmoid(pre_act)
    grad_pre = (grad_hidden * sigmoid_pre * (1.0 + pre_act * (1.0 - sigmoid_pre))).astype(
        jnp.bfloat16
    )
    grad_one = reduce_grad(
        lax.dot_general(patches_clip, grad_pre, contract_rows, preferred_element_type=jnp.float32)
    )
    student = output.astype(jnp.bfloat16).reshape(frames_n, height_n, width_n, chans)
    return (student, grad_one, grad_two)


def solution(mesh):
    in_specs = (
        P("tm", "height", None, None),
        P("tm", "height", None, None),
        P("height", None),
        P("height", None),
    )
    out_specs = (P("tm", "height", None, None), P("height", None), P("height", None))
    return jax.shard_map(shards, mesh=mesh, in_specs=in_specs, out_specs=out_specs, check_vma=False)
```

profile of v0, /device:TPU:0, one launch (start us, length us, event | category | flops | bytes accessed | tf_op | source)
XLA Modules:
  0.0 475.6 jit_solution(719828073563204116)
XLA Ops:
  7.9 2.4 collective-permute-start
  13.0 4.2 collective-permute-start.1
  19.8 4.1 collective-permute-done.2
  26.5 23.9 %copy.7 = bf16[2,8,48,27,256]{4,3,2,1,0:T(8,128)(2,1)S(1)} copy(bf16[2,8,48,27,256]{4,2,1,0,3:T(8,128)(2,1)S(1)} %bitcast_dynamic-update-slice_fusion.18) | data formatting | bytes 21233664 | tf_op jit(solution)/shard_map/stack | solution.py:61
  50.4 10.2 %copy.9 = bf16[96,8,27,256]{3,1,2,0:T(8,128)(2,1)} copy(bf16[96,8,27,256]{3,2,1,0:T(8,128)(2,1)S(1)} %bitcast.205) | data formatting | bytes 21233664
  60.6 23.9 %all-gather.3.cloned.1.call-done = bf16[6912,256]{1,0:T(8,128)(2,1)} async-done(((bf16[432,256]{1,0:T(8,128)(2,1)}), bf16[6912,256]{1,0:T(8,128)(2,1)}) %all-gather.3.cloned.1.call-update) | async-done | bytes 3538960 | tf_op jit(solution)/shard_map/all_gather | solution.py:90
  84.5 8.8 %multiply_convert_fusion = (bf16[768,256]{1,0:T(8,128)(2,1)S(1)}, f32[768,256]{1,0:T(8,128)}) fusion(bf16[768,6912]{1,0:T(8,128)(2,1)} %bitcast.207, bf16[6912,256]{1,0:T(8,128)(2,1)} %all-gather.3.cloned.1.call-done), kind=kOutput, calls=%fused_computation.16 | convolution fusion | flops 2718892032 | bytes 15335424 | tf_op jit(solution)/shard_map/dot_general | solution.py:92
  95.9 3.4 collective-permute-start.4
  101.8 4.1 collective-permute-done.5
  108.6 23.9 %copy.8 = bf16[2,8,48,27,256]{4,3,2,1,0:T(8,128)(2,1)S(1)} copy(bf16[2,8,48,27,256]{4,2,1,0,3:T(8,128)(2,1)S(1)} %bitcast_dynamic-update-slice_fusion) | data formatting | bytes 21233664 | tf_op jit(solution)/shard_map/stack | solution.py:61
  132.5 10.2 %copy.10 = bf16[96,8,27,256]{3,1,2,0:T(8,128)(2,1)} copy(bf16[96,8,27,256]{3,2,1,0:T(8,128)(2,1)S(1)} %bitcast.206) | data formatting | bytes 21233664
  142.7 14.7 %all-gather.5.cloned.1.call-done = bf16[6912,256]{1,0:T(8,128)(2,1)} async-done(((bf16[432,256]{1,0:T(8,128)(2,1)}), bf16[6912,256]{1,0:T(8,128)(2,1)}) %all-gather.5.cloned.1.call-update) | async-done | bytes 3538960 | tf_op jit(solution)/shard_map/all_gather | solution.py:94
  157.4 8.8 %fusion.4 = (bf16[768,256]{1,0:T(8,128)(2,1)S(1)}, bf16[768,256]{1,0:T(8,128)(2,1)}) fusion(bf16[2,8,48,256]{3,2,1,0:T(8,128)(2,1)S(1)} %copy-done.2, bf16[768,6912]{1,0:T(8,128)(2,1)} %bitcast.209, bf16[6912,256]{1,0:T(8,128)(2,1)} %all-gather.5.cloned.1.call-done, bf16[768,256]{1,0:T(8,128)(2,1)S(1)} %bitcast.246), kind=kOutput, calls=%fused_computation.12 | convolution fusion | flops 2719285248 | bytes 15728640 | tf_op jit(solution)/shard_map/dot_general | solution.py:96
  167.6 4.5 convolution_convert_fusion
  172.2 3.4 collective-permute-start.7
  175.5 1.5 collective-permute-start.8
  178.5 6.1 %collective-permute-done.8 = bf16[4,1,48,256]{3,2,1,0:T(8,128)(2,1)S(1)} collective-permute-done((bf16[4,1,48,256]{3,2,1,0:T(8,128)(2,1)S(1)}, bf16[4,1,48,256]{3,2,1,0:T(8,128)(2,1)S(1)}, u32[]{:S(2)}, u32[]{:S(2)}) %collective-permute-start.8) | collective-permute-done | bytes 98336 | tf_op jit(solution)/shard_map/ppermute | solution.py:24
  186.6 4.0 pad_slice_fusion
  210.2 20.4 %convolution_convert_fusion.1 = bf16[6912,256]{1,0:T(8,128)(2,1)} fusion(bf16[768,6912]{1,0:T(8,128)(2,1)} %bitcast.208, bf16[768,27,256]{2,0,1:T(8,128)(2,1)} %constant_dynamic-update-slice_fusion.2, bf16[27,256,256]{2,1,0:T(8,128)(2,1)S(1)} %bitcast.247, f32[768,256]{1,0:T(8,128)} %get-tuple-element.41), kind=kOutput, calls=%fused_computation.1 | convolution fusion | flops 5439356928 | bytes 29097984 | tf_op jit(solution)/shard_map/dot_general | solution.py:119
  230.6 75.9 %reduce-scatter.5.cloned.1.call-done = bf16[432,256]{1,0:T(8,128)(2,1)} async-done(((bf16[6912,256]{1,0:T(8,128)(2,1)}), bf16[432,256]{1,0:T(8,128)(2,1)}) %reduce-scatter.5.cloned.1.call-update) | async-done | bytes 221200 | tf_op jit(solution)/shard_map/reduce_scatter | solution.py:82
  306.6 139.2 %reduce-scatter.3.cloned.1.call-done = bf16[432,256]{1,0:T(8,128)(2,1)} async-done(((bf16[6912,256]{1,0:T(8,128)(2,1)}), bf16[432,256]{1,0:T(8,128)(2,1)}) %reduce-scatter.3.cloned.1.call-update) | async-done | bytes 221200 | tf_op jit(solution)/shard_map/reduce_scatter | solution.py:82
  445.8 19.8 %all-reduce.6.cloned.1.call-done = (bf16[432,256]{1,0:T(8,128)(2,1)}, bf16[432,256]{1,0:T(8,128)(2,1)}) async-done(((bf16[432,256]{1,0:T(8,128)(2,1)}, bf16[432,256]{1,0:T(8,128)(2,1)}), (bf16[432,256]{1,0:T(8,128)(2,1)}, bf16[432,256]{1,0:T(8,128)(2,1)})) %all-reduce.6.cloned.1.call-update) | async-done | bytes 442384 | tf_op jit(solution)/shard_map/psum | solution.py:85
  465.6 1.7 convert_element_type.49
  467.3 1.7 convert_element_type.51
  (124 shorter events, 40.5 us)
Async XLA Ops:
  7.2 77.3 %all-gather.3.cloned.1.call-start = ((), (), s32[]{:S(2)}) async-start(), calls=%async_computation.2 | async-start | bytes 3760128 | tf_op jit(solution)/shard_map/all_gather | solution.py:90
  7.9 149.5 %all-gather.5.cloned.1.call-start = ((), (), s32[]{:S(2)}) async-start(), calls=%async_computation.3 | async-start | bytes 3760128 | tf_op jit(solution)/shard_map/all_gather | solution.py:94
  7.9 3.9 collective-permute-start
  10.4 296.2 %reduce-scatter.5.cloned.1.call-start = ((), (), s32[]{:S(2)}) async-start(), calls=%async_computation.5 | async-start | bytes 3760128 | tf_op jit(solution)/shard_map/reduce_scatter | solution.py:82
  13.0 6.8 %collective-permute-start.1 = (bf16[4,1,48,256]{3,2,1,0:T(8,128)(2,1)S(1)}, bf16[4,1,48,256]{3,2,1,0:T(8,128)(2,1)S(1)}, u32[]{:S(2)}, u32[]{:S(2)}) collective-permute-start(bf16[4,1,48,256]{3,2,1,0:T(8,128)(2,1)S(1)} %get-tuple-element.38), channel_id=1, source_target_pairs={{0,1},{1,2},{2,3},{3,4},{4,5},{5,6},{6,7},{7,8},{8,9},{9,10},{10,1... | collective-permute-start | bytes 294920 | tf_op jit(solution)/shard_map/ppermute | solution.py:22
  17.2 6.7 %collective-permute-start.2 = (bf16[4,1,48,256]{3,2,1,0:T(8,128)(2,1)S(1)}, bf16[4,1,48,256]{3,2,1,0:T(8,128)(2,1)S(1)}, u32[]{:S(2)}, u32[]{:S(2)}) collective-permute-start(bf16[4,1,48,256]{3,2,1,0:T(8,128)(2,1)S(1)} %get-tuple-element.39), channel_id=1, source_target_pairs={{1,0},{2,1},{3,2},{4,3},{5,4},{6,5},{7,6},{8,7},{9,8},{10,9},{11,1... | collective-permute-start | bytes 294920 | tf_op jit(solution)/shard_map/ppermute | solution.py:24
  93.3 2.6 collective-permute-start.3
  95.9 5.9 %collective-permute-start.4 = (bf16[4,1,48,256]{3,2,1,0:T(8,128)(2,1)S(1)}, bf16[4,1,48,256]{3,2,1,0:T(8,128)(2,1)S(1)}, u32[]{:S(2)}, u32[]{:S(2)}) collective-permute-start(bf16[4,1,48,256]{3,2,1,0:T(8,128)(2,1)S(1)} %get-tuple-element.36), channel_id=1, source_target_pairs={{0,1},{1,2},{2,3},{3,4},{4,5},{5,6},{6,7},{7,8},{8,9},{9,10},{10,1... | collective-permute-start | bytes 294920 | tf_op jit(solution)/shard_map/ppermute | solution.py:22
  99.3 6.7 %collective-permute-start.5 = (bf16[4,1,48,256]{3,2,1,0:T(8,128)(2,1)S(1)}, bf16[4,1,48,256]{3,2,1,0:T(8,128)(2,1)S(1)}, u32[]{:S(2)}, u32[]{:S(2)}) collective-permute-start(bf16[4,1,48,256]{3,2,1,0:T(8,128)(2,1)S(1)} %get-tuple-element.37), channel_id=1, source_target_pairs={{1,0},{2,1},{3,2},{4,3},{5,4},{6,5},{7,6},{8,7},{9,8},{10,9},{11,1... | collective-permute-start | bytes 294920 | tf_op jit(solution)/shard_map/ppermute | solution.py:24
  132.5 24.9 %copy-start = (bf16[2,8,48,256]{3,2,1,0:T(8,128)(2,1)S(1)}, bf16[2,8,48,256]{3,2,1,0:T(8,128)(2,1)}, u32[]{:S(2)}) copy-start(bf16[2,8,48,256]{3,2,1,0:T(8,128)(2,1)} %param.4) | copy-start | bytes 1179652
  132.5 24.9 %copy-start.2 = (bf16[2,8,48,256]{3,2,1,0:T(8,128)(2,1)S(1)}, bf16[2,8,48,256]{3,2,1,0:T(8,128)(2,1)}, u32[]{:S(2)}) copy-start(bf16[2,8,48,256]{3,2,1,0:T(8,128)(2,1)} %param.5) | copy-start | bytes 1179652
  142.7 24.8 %slice-start = ((s8[10616832]{0:T(1024)(128)(4,1)}), s8[2228224]{0:T(1024)(128)(4,1)S(1)}, s32[]{:S(2)}) async-start(s8[10616832]{0:T(1024)(128)(4,1)} %bitcast.210), calls=%async_computation.7 | async-start | bytes 4456448
  157.4 10.1 %slice-start.1 = ((s8[10616832]{0:T(1024)(128)(4,1)}), s8[4194304]{0:T(1024)(128)(4,1)S(1)}, s32[]{:S(2)}) async-start(s8[10616832]{0:T(1024)(128)(4,1)} %bitcast.210), calls=%async_computation.8 | async-start | bytes 8388608
  157.4 10.1 %slice-start.2 = ((s8[10616832]{0:T(1024)(128)(4,1)}), s8[4194304]{0:T(1024)(128)(4,1)S(1)}, s32[]{:S(2)}) async-start(s8[10616832]{0:T(1024)(128)(4,1)} %bitcast.210), calls=%async_computation.9 | async-start | bytes 8388608
  166.2 5.9 %collective-permute-start.6 = (bf16[2,8,48,256]{3,2,1,0:T(8,128)(2,1)S(1)}, bf16[2,8,48,256]{3,2,1,0:T(8,128)(2,1)S(1)}, u32[]{:S(2)}, u32[]{:S(2)}) collective-permute-start(bf16[2,8,48,256]{3,2,1,0:T(8,128)(2,1)S(1)} %bitcast.232), channel_id=1, source_target_pairs={{16,0},{17,1},{18,2},{19,3},{20,4},{21,5},{22,6},{23,7},{24,8},{25... | collective-permute-start | bytes 1179656 | tf_op jit(solution)/shard_map/ppermute | solution.py:11
  172.1 273.7 %reduce-scatter.3.cloned.1.call-start = ((), (), s32[]{:S(2)}) async-start(), calls=%async_computation.4 | async-start | bytes 3760128 | tf_op jit(solution)/shard_map/reduce_scatter | solution.py:82
  172.2 6.3 %collective-permute-start.7 = (bf16[4,1,48,256]{3,2,1,0:T(8,128)(2,1)S(1)}, bf16[4,1,48,256]{3,2,1,0:T(8,128)(2,1)S(1)}, u32[]{:S(2)}, u32[]{:S(2)}) collective-permute-start(bf16[4,1,48,256]{3,2,1,0:T(8,128)(2,1)S(1)} %get-tuple-element.32), channel_id=1, source_target_pairs={{0,1},{1,2},{2,3},{3,4},{4,5},{5,6},{6,7},{7,8},{8,9},{9,10},{10,1... | collective-permute-start | bytes 294920 | tf_op jit(solution)/shard_map/ppermute | solution.py:22
  175.5 9.0 %collective-permute-start.8 = (bf16[4,1,48,256]{3,2,1,0:T(8,128)(2,1)S(1)}, bf16[4,1,48,256]{3,2,1,0:T(8,128)(2,1)S(1)}, u32[]{:S(2)}, u32[]{:S(2)}) collective-permute-start(bf16[4,1,48,256]{3,2,1,0:T(8,128)(2,1)S(1)} %get-tuple-element.33), channel_id=1, source_target_pairs={{1,0},{2,1},{3,2},{4,3},{5,4},{6,5},{7,6},{8,7},{9,8},{10,9},{11,1... | collective-permute-start | bytes 294920 | tf_op jit(solution)/shard_map/ppermute | solution.py:24
  190.6 19.6 %copy-start.1 = (bf16[6912,256]{1,0:T(8,128)(2,1)S(1)}, bf16[6912,256]{1,0:T(8,128)(2,1)}, u32[]{:S(2)}) copy-start(bf16[6912,256]{1,0:T(8,128)(2,1)} %all-gather.5.cloned.1.call-done) | copy-start | bytes 10616836
  230.6 235.0 %all-reduce.6.cloned.1.call-start = ((), (), s32[]{:S(2)}) async-start(), calls=%async_computation.6 | async-start | bytes 884736 | tf_op jit(solution)/shard_map/psum | solution.py:85
Sparse Core Ops, SparseCore 0:
  10.8 73.6 all-gather.2
  87.3 70.1 all-gather.4
  172.2 134.3 reduce-scatter.4
  311.5 134.1 reduce-scatter.2
  448.0 17.5 all-reduce.5
where the time goes:
time: 476 us
  waiting for transfers between devices  295 us (62%)
  local copies, waits for them, and re-layouts  99.1 us (21%)
  matrix products  42.5 us (9%)
  starting transfers between devices  20.4 us (4%)
  between operations  14.3 us (3%)
    reduce_scatter x2, waiting for transfers between devices, reduce_grad(): lax.psum_scatter(local_grad.astype(jnp.bfloat16), 'height', scatter_dimen...  215 us
    another operation x4, local copies, waits for them, and re-layouts, causal_patches(): jnp.stack(pieces, axis=3).reshape(frames_n * height_n * width_n, 27 * chans)  47.9 us
    unnamed x93, local copies, waits for them, and re-layouts  45.1 us
    all_gather x1, waiting for transfers between devices, shards(): full_one = lax.all_gather(kernel_one, 'height', axis=0, tiled=True)  23.9 us
    dot_general x1, matrix products, shards(): lax.dot_general(patches_clip, grad_pre, contract_rows, preferred_element_...  20.4 us
    psum x1, waiting for transfers between devices, reduce_grad(): return lax.psum(owned, 'tm').astype(jnp.float32)  19.8 us
    all_gather x1, waiting for transfers between devices, shards(): full_two = lax.all_gather(kernel_two, 'height', axis=0, tiled=True)  14.7 us
    ppermute x3, waiting for transfers between devices, extended_2(): lax.ppermute(head, axis, [((i + 1) % count, i) for i in range(ends)])  14.3 us
  transfers between devices with their start and end apart: 14, of which 13 were waited for; matrix products, arithmetic and copies ran while one was open for 28% of the time, Pallas kernels for 0%

commit v1 on v0

--- a/solution.py
+++ b/solution.py
@@ -3,6 +3,12 @@
 import jax.numpy as jnp
 from jax import lax
 from jax.sharding import PartitionSpec as P
+
+
+def laid_out(parts, dim):
+    parts = jnp.moveaxis(parts, 0, dim)
+    shape = parts.shape
+    return parts.reshape(*shape[:dim], shape[dim] * shape[dim + 1], *shape[dim + 2 :])
 
 
 def shifted(value, axis, by):
@@ -87,7 +93,14 @@
 
 def shards(clip, teacher, kernel_one, kernel_two):
     frames_n, height_n, width_n, chans = clip.shape
-    full_one = lax.all_gather(kernel_one, "height", axis=0, tiled=True)
+    size = lax.axis_size("height")
+    right = [(i_2, (i_2 + 1) % size) for i_2 in range(size)]
+    blocks_2 = [kernel_one]
+    while len(blocks_2) < size:
+        blocks_2.append(lax.ppermute(blocks_2[-1], "height", right))
+    index = lax.axis_index("height")
+    blocks_2 = jnp.stack(blocks_2)[(index - jnp.arange(size)) % size]
+    full_one = laid_out(blocks_2, 0)
     patches_clip = causal_patches(clip)
     pre_act = jnp.dot(patches_clip, full_one, preferred_element_type=jnp.float32)
     hidden = jax.nn.silu(pre_act).astype(jnp.bfloat16)

time: 476 us -> 573 us (1.20)
  waiting for transfers between devices: 295 us -> 404 us
  local copies, waits for them, and re-layouts: 99.1 us -> 88.6 us
    ppermute x0 -> x15, waiting for transfers between devices: none -> 138 us  [shards(): blocks_2.append(lax.ppermute(blocks_2[-1], 'height', right))]
    all_gather x1 -> x0, waiting for transfers between devices: 23.9 us -> none  [shards(): full_one = lax.all_gather(kernel_one, 'height', axis=0, tiled=True)]
    reduce_scatter x2, waiting for transfers between devices: 215 us -> 231 us  [reduce_grad(): lax.psum_scatter(local_grad.astype(jnp.bfloat16), 'height', scatter_dimen...]
    all_gather x1, waiting for transfers between devices: 14.7 us -> 0.01 us  [shards(): full_two = lax.all_gather(kernel_two, 'height', axis=0, tiled=True)]
    unnamed x93 -> x110, local copies, waits for them, and re-layouts: 45.1 us -> 32.6 us
    ppermute x3, starting transfers between devices: 10.9 us -> 4.8 us  [extended_2(): lax.ppermute(tail, axis, [(i, (i + 1) % count) for i in range(ends)])]
  transfers between devices with their start and end apart: 14 -> 28, of which waited for: 13 -> 22; matrix products, arithmetic and copies ran while one was open for 28% -> 21% of each run, Pallas kernels for 0% -> 0%
where the time goes in v1:
time: 573 us; the launch traced here: 572 us
  waiting for transfers between devices  404 us (71%)
  local copies, waits for them, and re-layouts  88.6 us (15%)
  matrix products  42.4 us (7%)
  starting transfers between devices  18.6 us (3%)
  between operations  14.7 us (3%)
    reduce_scatter x2, waiting for transfers between devices, reduce_grad(): lax.psum_scatter(local_grad.astype(jnp.bfloat16), 'height', scatter_dimen...  231 us
    ppermute x15, waiting for transfers between devices, shards(): blocks_2.append(lax.ppermute(blocks_2[-1], 'height', right))  138 us
    another operation x4, local copies, waits for them, and re-layouts, causal_patches(): jnp.stack(pieces, axis=3).reshape(frames_n * height_n * width_n, 27 * chans)  47.9 us
    unnamed x110, local copies, waits for them, and re-layouts  32.6 us
    dot_general x1, matrix products, shards(): lax.dot_general(patches_clip, grad_pre, contract_rows, preferred_element_...  20.3 us
    psum x1, waiting for transfers between devices, reduce_grad(): return lax.psum(owned, 'tm').astype(jnp.float32)  19.8 us
  transfers between devices with their start and end apart: 28, of which 22 were waited for; matrix products, arithmetic and copies ran while one was open for 21% of the time, Pallas kernels for 0%

profile of v1, /device:TPU:0, one launch (start us, length us, event | category | flops | bytes accessed | tf_op | source)
XLA Modules:
  0.0 572.4 jit_solution(14651005296974437553)
XLA Ops:
  13.8 7.5 %collective-permute-done.3 = bf16[432,256]{1,0:T(8,128)(2,1)} collective-permute-done((bf16[432,256]{1,0:T(8,128)(2,1)}, bf16[432,256]{1,0:T(8,128)(2,1)}, u32[]{:S(2)}, u32[]{:S(2)}) %collective-permute-start.3) | collective-permute-done | bytes 221216 | tf_op jit(solution)/shard_map/ppermute | solution.py:100
  27.7 6.9 %collective-permute-done.4 = bf16[432,256]{1,0:T(8,128)(2,1)S(1)} collective-permute-done((bf16[432,256]{1,0:T(8,128)(2,1)}, bf16[432,256]{1,0:T(8,128)(2,1)S(1)}, u32[]{:S(2)}, u32[]{:S(2)}) %collective-permute-start.4) | collective-permute-done | bytes 221216 | tf_op jit(solution)/shard_map/ppermute | solution.py:100
  37.3 23.9 %copy.7 = bf16[2,8,48,27,256]{4,3,2,1,0:T(8,128)(2,1)S(1)} copy(bf16[2,8,48,27,256]{4,2,1,0,3:T(8,128)(2,1)S(1)} %bitcast_dynamic-update-slice_fusion.18) | data formatting | bytes 21233664 | tf_op jit(solution)/shard_map/stack | solution.py:67
  61.2 10.2 %copy.9 = bf16[96,8,27,256]{3,1,2,0:T(8,128)(2,1)} copy(bf16[96,8,27,256]{3,2,1,0:T(8,128)(2,1)S(1)} %bitcast.240) | data formatting | bytes 21233664
  72.7 14.2 %collective-permute-done.6 = bf16[432,256]{1,0:T(8,128)(2,1)S(1)} collective-permute-done((bf16[432,256]{1,0:T(8,128)(2,1)S(1)}, bf16[432,256]{1,0:T(8,128)(2,1)S(1)}, u32[]{:S(2)}, u32[]{:S(2)}) %collective-permute-start.6) | collective-permute-done | bytes 221216 | tf_op jit(solution)/shard_map/ppermute | solution.py:100
  86.9 9.5 %collective-permute-done.7 = bf16[432,256]{1,0:T(8,128)(2,1)S(1)} collective-permute-done((bf16[432,256]{1,0:T(8,128)(2,1)S(1)}, bf16[432,256]{1,0:T(8,128)(2,1)S(1)}, u32[]{:S(2)}, u32[]{:S(2)}) %collective-permute-start.7) | collective-permute-done | bytes 221216 | tf_op jit(solution)/shard_map/ppermute | solution.py:100
  96.5 9.5 %collective-permute-done.8 = bf16[432,256]{1,0:T(8,128)(2,1)S(1)} collective-permute-done((bf16[432,256]{1,0:T(8,128)(2,1)S(1)}, bf16[432,256]{1,0:T(8,128)(2,1)S(1)}, u32[]{:S(2)}, u32[]{:S(2)}) %collective-permute-start.8) | collective-permute-done | bytes 221216 | tf_op jit(solution)/shard_map/ppermute | solution.py:100
  106.0 9.5 %collective-permute-done.9 = bf16[432,256]{1,0:T(8,128)(2,1)S(1)} collective-permute-done((bf16[432,256]{1,0:T(8,128)(2,1)S(1)}, bf16[432,256]{1,0:T(8,128)(2,1)S(1)}, u32[]{:S(2)}, u32[]{:S(2)}) %collective-permute-start.9) | collective-permute-done | bytes 221216 | tf_op jit(solution)/shard_map/ppermute | solution.py:100
  115.5 10.3 %collective-permute-done.10 = bf16[432,256]{1,0:T(8,128)(2,1)S(1)} collective-permute-done((bf16[432,256]{1,0:T(8,128)(2,1)S(1)}, bf16[432,256]{1,0:T(8,128)(2,1)S(1)}, u32[]{:S(2)}, u32[]{:S(2)}) %collective-permute-start.10) | collective-permute-done | bytes 221216 | tf_op jit(solution)/shard_map/ppermute | solution.py:100
  125.8 11.4 %collective-permute-done.11 = bf16[432,256]{1,0:T(8,128)(2,1)S(1)} collective-permute-done((bf16[432,256]{1,0:T(8,128)(2,1)S(1)}, bf16[432,256]{1,0:T(8,128)(2,1)S(1)}, u32[]{:S(2)}, u32[]{:S(2)}) %collective-permute-start.11) | collective-permute-done | bytes 221216 | tf_op jit(solution)/shard_map/ppermute | solution.py:100
  137.2 11.2 %collective-permute-done.12 = bf16[432,256]{1,0:T(8,128)(2,1)S(1)} collective-permute-done((bf16[432,256]{1,0:T(8,128)(2,1)S(1)}, bf16[432,256]{1,0:T(8,128)(2,1)S(1)}, u32[]{:S(2)}, u32[]{:S(2)}) %collective-permute-start.12) | collective-permute-done | bytes 221216 | tf_op jit(solution)/shard_map/ppermute | solution.py:100
  148.5 10.3 %collective-permute-done.13 = bf16[432,256]{1,0:T(8,128)(2,1)S(1)} collective-permute-done((bf16[432,256]{1,0:T(8,128)(2,1)S(1)}, bf16[432,256]{1,0:T(8,128)(2,1)S(1)}, u32[]{:S(2)}, u32[]{:S(2)}) %collective-permute-start.13) | collective-permute-done | bytes 221216 | tf_op jit(solution)/shard_map/ppermute | solution.py:100
  158.8 9.5 %collective-permute-done.14 = bf16[432,256]{1,0:T(8,128)(2,1)S(1)} collective-permute-done((bf16[432,256]{1,0:T(8,128)(2,1)S(1)}, bf16[432,256]{1,0:T(8,128)(2,1)S(1)}, u32[]{:S(2)}, u32[]{:S(2)}) %collective-permute-start.14) | collective-permute-done | bytes 221216 | tf_op jit(solution)/shard_map/ppermute | solution.py:100
  168.3 9.5 %collective-permute-done.15 = bf16[432,256]{1,0:T(8,128)(2,1)S(1)} collective-permute-done((bf16[432,256]{1,0:T(8,128)(2,1)S(1)}, bf16[432,256]{1,0:T(8,128)(2,1)S(1)}, u32[]{:S(2)}, u32[]{:S(2)}) %collective-permute-start.15) | collective-permute-done | bytes 221216 | tf_op jit(solution)/shard_map/ppermute | solution.py:100
  177.9 9.5 %collective-permute-done.16 = bf16[432,256]{1,0:T(8,128)(2,1)S(1)} collective-permute-done((bf16[432,256]{1,0:T(8,128)(2,1)S(1)}, bf16[432,256]{1,0:T(8,128)(2,1)S(1)}, u32[]{:S(2)}, u32[]{:S(2)}) %collective-permute-start.16) | collective-permute-done | bytes 221216 | tf_op jit(solution)/shard_map/ppermute | solution.py:100
  187.4 9.5 %collective-permute-done.17 = bf16[432,256]{1,0:T(8,128)(2,1)S(1)} collective-permute-done((bf16[432,256]{1,0:T(8,128)(2,1)S(1)}, bf16[432,256]{1,0:T(8,128)(2,1)S(1)}, u32[]{:S(2)}, u32[]{:S(2)}) %collective-permute-start.17) | collective-permute-done | bytes 221216 | tf_op jit(solution)/shard_map/ppermute | solution.py:100
  199.5 8.8 %multiply_convert_fusion = (bf16[768,256]{1,0:T(8,128)(2,1)S(1)}, f32[768,256]{1,0:T(8,128)}) fusion(bf16[768,6912]{1,0:T(8,128)(2,1)} %bitcast.242, bf16[6912,256]{1,0:T(8,128)(2,1)} %bitcast.248), kind=kOutput, calls=%fused_computation.17 | convolution fusion | flops 2718892032 | bytes 15335424 | tf_op jit(solution)/shard_map/dot_general | solution.py:105
  222.0 23.9 %copy.8 = bf16[2,8,48,27,256]{4,3,2,1,0:T(8,128)(2,1)S(1)} copy(bf16[2,8,48,27,256]{4,2,1,0,3:T(8,128)(2,1)S(1)} %bitcast_dynamic-update-slice_fusion) | data formatting | bytes 21233664 | tf_op jit(solution)/shard_map/stack | solution.py:67
  245.9 10.2 %copy.10 = bf16[96,8,27,256]{3,1,2,0:T(8,128)(2,1)} copy(bf16[96,8,27,256]{3,2,1,0:T(8,128)(2,1)S(1)} %bitcast.241) | data formatting | bytes 21233664
  256.1 8.8 %fusion.4 = (bf16[768,256]{1,0:T(8,128)(2,1)S(1)}, bf16[768,256]{1,0:T(8,128)(2,1)}) fusion(bf16[2,8,48,256]{3,2,1,0:T(8,128)(2,1)S(1)} %copy-done.3, bf16[768,6912]{1,0:T(8,128)(2,1)} %bitcast.244, bf16[6912,256]{1,0:T(8,128)(2,1)} %all-gather.2.cloned.1.call-done, bf16[768,256]{1,0:T(8,128)(2,1)S(1)} %bitcast.282), kind=kOutput, calls=%fused_computation.13 | convolution fusion | flops 2719285248 | bytes 15728640 | tf_op jit(solution)/shard_map/dot_general | solution.py:109
  290.8 20.3 %convolution_convert_fusion.1 = bf16[6912,256]{1,0:T(8,128)(2,1)} fusion(bf16[768,6912]{1,0:T(8,128)(2,1)} %bitcast.243, bf16[768,27,256]{2,0,1:T(8,128)(2,1)} %copy-done.1, bf16[27,256,256]{2,1,0:T(8,128)(2,1)S(1)} %bitcast.283, f32[768,256]{1,0:T(8,128)} %get-tuple-element.41), kind=kOutput, calls=%fused_computation.2 | convolution fusion | flops 5439356928 | bytes 29097984 | tf_op jit(solution)/shard_map/dot_general | solution.py:132
  311.1 91.9 %reduce-scatter.5.cloned.1.call-done = bf16[432,256]{1,0:T(8,128)(2,1)} async-done(((bf16[6912,256]{1,0:T(8,128)(2,1)}), bf16[432,256]{1,0:T(8,128)(2,1)}) %reduce-scatter.5.cloned.1.call-update) | async-done | bytes 221200 | tf_op jit(solution)/shard_map/reduce_scatter | solution.py:88
  403.0 139.5 %reduce-scatter.3.cloned.1.call-done = bf16[432,256]{1,0:T(8,128)(2,1)} async-done(((bf16[6912,256]{1,0:T(8,128)(2,1)}), bf16[432,256]{1,0:T(8,128)(2,1)}) %reduce-scatter.3.cloned.1.call-update) | async-done | bytes 221200 | tf_op jit(solution)/shard_map/reduce_scatter | solution.py:88
  542.6 19.8 %all-reduce.6.cloned.1.call-done = (bf16[432,256]{1,0:T(8,128)(2,1)}, bf16[432,256]{1,0:T(8,128)(2,1)}) async-done(((bf16[432,256]{1,0:T(8,128)(2,1)}, bf16[432,256]{1,0:T(8,128)(2,1)}), (bf16[432,256]{1,0:T(8,128)(2,1)}, bf16[432,256]{1,0:T(8,128)(2,1)})) %all-reduce.6.cloned.1.call-update) | async-done | bytes 442384 | tf_op jit(solution)/shard_map/psum | solution.py:91
  (172 shorter events, 62.0 us)
Async XLA Ops:
  7.2 249.0 %all-gather.2.cloned.1.call-start = ((), (), s32[]{:S(2)}) async-start(), calls=%async_computation.2 | async-start | bytes 3760128 | tf_op jit(solution)/shard_map/all_gather | solution.py:107
  7.2 15.1 %collective-permute-start = (bf16[2,8,48,256]{3,2,1,0:T(8,128)(2,1)}, bf16[2,8,48,256]{3,2,1,0:T(8,128)(2,1)}, u32[]{:S(2)}, u32[]{:S(2)}) collective-permute-start(bf16[2,8,48,256]{3,2,1,0:T(8,128)(2,1)} %param.4), channel_id=1, source_target_pairs={{0,16},{1,17},{2,18},{3,19},{4,20},{5,21},{6,22},{7,23},{8,24},{9,... | collective-permute-start | bytes 1179656 | tf_op jit(solution)/shard_map/ppermute | solution.py:17
  10.4 10.9 %collective-permute-start.3 = (bf16[432,256]{1,0:T(8,128)(2,1)}, bf16[432,256]{1,0:T(8,128)(2,1)}, u32[]{:S(2)}, u32[]{:S(2)}) collective-permute-start(bf16[432,256]{1,0:T(8,128)(2,1)} %param.6), channel_id=1, source_target_pairs={{0,1},{1,2},{2,3},{3,4},{4,5},{5,6},{6,7},{7,8},{8,9},{9,10},{10,1... | collective-permute-start | bytes 663560 | tf_op jit(solution)/shard_map/ppermute | solution.py:100
  12.7 390.3 %reduce-scatter.5.cloned.1.call-start = ((), (), s32[]{:S(2)}) async-start(), calls=%async_computation.4 | async-start | bytes 3760128 | tf_op jit(solution)/shard_map/reduce_scatter | solution.py:88
  21.3 13.4 %collective-permute-start.4 = (bf16[432,256]{1,0:T(8,128)(2,1)}, bf16[432,256]{1,0:T(8,128)(2,1)S(1)}, u32[]{:S(2)}, u32[]{:S(2)}) collective-permute-start(bf16[432,256]{1,0:T(8,128)(2,1)} %collective-permute-done.3), channel_id=1, source_target_pairs={{0,1},{1,2},{2,3},{3,4},{4,5},{5,6},{6,7},{7,8},{8,9},{9,10},{10,1... | collective-permute-start | bytes 663560 | tf_op jit(solution)/shard_map/ppermute | solution.py:100
  24.4 10.3 %collective-permute-start.1 = (bf16[4,1,48,256]{3,2,1,0:T(8,128)(2,1)S(1)}, bf16[4,1,48,256]{3,2,1,0:T(8,128)(2,1)S(1)}, u32[]{:S(2)}, u32[]{:S(2)}) collective-permute-start(bf16[4,1,48,256]{3,2,1,0:T(8,128)(2,1)S(1)} %get-tuple-element.38), channel_id=1, source_target_pairs={{0,1},{1,2},{2,3},{3,4},{4,5},{5,6},{6,7},{7,8},{8,9},{9,10},{10,1... | collective-permute-start | bytes 294920 | tf_op jit(solution)/shard_map/ppermute | solution.py:28
  26.4 8.3 %collective-permute-start.2 = (bf16[4,1,48,256]{3,2,1,0:T(8,128)(2,1)S(1)}, bf16[4,1,48,256]{3,2,1,0:T(8,128)(2,1)S(1)}, u32[]{:S(2)}, u32[]{:S(2)}) collective-permute-start(bf16[4,1,48,256]{3,2,1,0:T(8,128)(2,1)S(1)} %get-tuple-element.39), channel_id=1, source_target_pairs={{1,0},{2,1},{3,2},{4,3},{5,4},{6,5},{7,6},{8,7},{9,8},{10,9},{11,1... | collective-permute-start | bytes 294920 | tf_op jit(solution)/shard_map/ppermute | solution.py:30
  34.7 36.7 %collective-permute-start.5 = (bf16[432,256]{1,0:T(8,128)(2,1)S(1)}, bf16[432,256]{1,0:T(8,128)(2,1)S(1)}, u32[]{:S(2)}, u32[]{:S(2)}) collective-permute-start(bf16[432,256]{1,0:T(8,128)(2,1)S(1)} %collective-permute-done.4), channel_id=1, source_target_pairs={{0,1},{1,2},{2,3},{3,4},{4,5},{5,6},{6,7},{7,8},{8,9},{9,10},{10,1... | collective-permute-start | bytes 663560 | tf_op jit(solution)/shard_map/ppermute | solution.py:100
  71.4 15.5 %collective-permute-start.6 = (bf16[432,256]{1,0:T(8,128)(2,1)S(1)}, bf16[432,256]{1,0:T(8,128)(2,1)S(1)}, u32[]{:S(2)}, u32[]{:S(2)}) collective-permute-start(bf16[432,256]{1,0:T(8,128)(2,1)S(1)} %collective-permute-done.5), channel_id=1, source_target_pairs={{0,1},{1,2},{2,3},{3,4},{4,5},{5,6},{6,7},{7,8},{8,9},{9,10},{10,1... | collective-permute-start | bytes 663560 | tf_op jit(solution)/shard_map/ppermute | solution.py:100
  86.9 9.5 %collective-permute-start.7 = (bf16[432,256]{1,0:T(8,128)(2,1)S(1)}, bf16[432,256]{1,0:T(8,128)(2,1)S(1)}, u32[]{:S(2)}, u32[]{:S(2)}) collective-permute-start(bf16[432,256]{1,0:T(8,128)(2,1)S(1)} %collective-permute-done.6), channel_id=1, source_target_pairs={{0,1},{1,2},{2,3},{3,4},{4,5},{5,6},{6,7},{7,8},{8,9},{9,10},{10,1... | collective-permute-start | bytes 663560 | tf_op jit(solution)/shard_map/ppermute | solution.py:100
  96.4 9.5 %collective-permute-start.8 = (bf16[432,256]{1,0:T(8,128)(2,1)S(1)}, bf16[432,256]{1,0:T(8,128)(2,1)S(1)}, u32[]{:S(2)}, u32[]{:S(2)}) collective-permute-start(bf16[432,256]{1,0:T(8,128)(2,1)S(1)} %collective-permute-done.7), channel_id=1, source_target_pairs={{0,1},{1,2},{2,3},{3,4},{4,5},{5,6},{6,7},{7,8},{8,9},{9,10},{10,1... | collective-permute-start | bytes 663560 | tf_op jit(solution)/shard_map/ppermute | solution.py:100
  106.0 9.5 %collective-permute-start.9 = (bf16[432,256]{1,0:T(8,128)(2,1)S(1)}, bf16[432,256]{1,0:T(8,128)(2,1)S(1)}, u32[]{:S(2)}, u32[]{:S(2)}) collective-permute-start(bf16[432,256]{1,0:T(8,128)(2,1)S(1)} %collective-permute-done.8), channel_id=1, source_target_pairs={{0,1},{1,2},{2,3},{3,4},{4,5},{5,6},{6,7},{7,8},{8,9},{9,10},{10,1... | collective-permute-start | bytes 663560 | tf_op jit(solution)/shard_map/ppermute | solution.py:100
  115.5 10.3 %collective-permute-start.10 = (bf16[432,256]{1,0:T(8,128)(2,1)S(1)}, bf16[432,256]{1,0:T(8,128)(2,1)S(1)}, u32[]{:S(2)}, u32[]{:S(2)}) collective-permute-start(bf16[432,256]{1,0:T(8,128)(2,1)S(1)} %collective-permute-done.9), channel_id=1, source_target_pairs={{0,1},{1,2},{2,3},{3,4},{4,5},{5,6},{6,7},{7,8},{8,9},{9,10},{10,1... | collective-permute-start | bytes 663560 | tf_op jit(solution)/shard_map/ppermute | solution.py:100
  125.8 11.4 %collective-permute-start.11 = (bf16[432,256]{1,0:T(8,128)(2,1)S(1)}, bf16[432,256]{1,0:T(8,128)(2,1)S(1)}, u32[]{:S(2)}, u32[]{:S(2)}) collective-permute-start(bf16[432,256]{1,0:T(8,128)(2,1)S(1)} %collective-permute-done.10), channel_id=1, source_target_pairs={{0,1},{1,2},{2,3},{3,4},{4,5},{5,6},{6,7},{7,8},{8,9},{9,10},{10,1... | collective-permute-start | bytes 663560 | tf_op jit(solution)/shard_map/ppermute | solution.py:100
  137.2 11.2 %collective-permute-start.12 = (bf16[432,256]{1,0:T(8,128)(2,1)S(1)}, bf16[432,256]{1,0:T(8,128)(2,1)S(1)}, u32[]{:S(2)}, u32[]{:S(2)}) collective-permute-start(bf16[432,256]{1,0:T(8,128)(2,1)S(1)} %collective-permute-done.11), channel_id=1, source_target_pairs={{0,1},{1,2},{2,3},{3,4},{4,5},{5,6},{6,7},{7,8},{8,9},{9,10},{10,1... | collective-permute-start | bytes 663560 | tf_op jit(solution)/shard_map/ppermute | solution.py:100
  148.4 10.4 %collective-permute-start.13 = (bf16[432,256]{1,0:T(8,128)(2,1)S(1)}, bf16[432,256]{1,0:T(8,128)(2,1)S(1)}, u32[]{:S(2)}, u32[]{:S(2)}) collective-permute-start(bf16[432,256]{1,0:T(8,128)(2,1)S(1)} %collective-permute-done.12), channel_id=1, source_target_pairs={{0,1},{1,2},{2,3},{3,4},{4,5},{5,6},{6,7},{7,8},{8,9},{9,10},{10,1... | collective-permute-start | bytes 663560 | tf_op jit(solution)/shard_map/ppermute | solution.py:100
  158.8 9.5 %collective-permute-start.14 = (bf16[432,256]{1,0:T(8,128)(2,1)S(1)}, bf16[432,256]{1,0:T(8,128)(2,1)S(1)}, u32[]{:S(2)}, u32[]{:S(2)}) collective-permute-start(bf16[432,256]{1,0:T(8,128)(2,1)S(1)} %collective-permute-done.13), channel_id=1, source_target_pairs={{0,1},{1,2},{2,3},{3,4},{4,5},{5,6},{6,7},{7,8},{8,9},{9,10},{10,1... | collective-permute-start | bytes 663560 | tf_op jit(solution)/shard_map/ppermute | solution.py:100
  168.3 9.5 %collective-permute-start.15 = (bf16[432,256]{1,0:T(8,128)(2,1)S(1)}, bf16[432,256]{1,0:T(8,128)(2,1)S(1)}, u32[]{:S(2)}, u32[]{:S(2)}) collective-permute-start(bf16[432,256]{1,0:T(8,128)(2,1)S(1)} %collective-permute-done.14), channel_id=1, source_target_pairs={{0,1},{1,2},{2,3},{3,4},{4,5},{5,6},{6,7},{7,8},{8,9},{9,10},{10,1... | collective-permute-start | bytes 663560 | tf_op jit(solution)/shard_map/ppermute | solution.py:100
  177.8 9.5 %collective-permute-start.16 = (bf16[432,256]{1,0:T(8,128)(2,1)S(1)}, bf16[432,256]{1,0:T(8,128)(2,1)S(1)}, u32[]{:S(2)}, u32[]{:S(2)}) collective-permute-start(bf16[432,256]{1,0:T(8,128)(2,1)S(1)} %collective-permute-done.15), channel_id=1, source_target_pairs={{0,1},{1,2},{2,3},{3,4},{4,5},{5,6},{6,7},{7,8},{8,9},{9,10},{10,1... | collective-permute-start | bytes 663560 | tf_op jit(solution)/shard_map/ppermute | solution.py:100
  187.4 9.5 %collective-permute-start.17 = (bf16[432,256]{1,0:T(8,128)(2,1)S(1)}, bf16[432,256]{1,0:T(8,128)(2,1)S(1)}, u32[]{:S(2)}, u32[]{:S(2)}) collective-permute-start(bf16[432,256]{1,0:T(8,128)(2,1)S(1)} %collective-permute-done.16), channel_id=1, source_target_pairs={{0,1},{1,2},{2,3},{3,4},{4,5},{5,6},{6,7},{7,8},{8,9},{9,10},{10,1... | collective-permute-start | bytes 663560 | tf_op jit(solution)/shard_map/ppermute | solution.py:100
  212.3 7.0 %collective-permute-start.20 = (bf16[4,1,48,256]{3,2,1,0:T(8,128)(2,1)S(1)}, bf16[4,1,48,256]{3,2,1,0:T(8,128)(2,1)S(1)}, u32[]{:S(2)}, u32[]{:S(2)}) collective-permute-start(bf16[4,1,48,256]{3,2,1,0:T(8,128)(2,1)S(1)} %get-tuple-element.37), channel_id=1, source_target_pairs={{1,0},{2,1},{3,2},{4,3},{5,4},{6,5},{7,6},{8,7},{9,8},{10,9},{11,1... | collective-permute-start | bytes 294920 | tf_op jit(solution)/shard_map/ppermute | solution.py:30
  270.8 271.8 %reduce-scatter.3.cloned.1.call-start = ((), (), s32[]{:S(2)}) async-start(), calls=%async_computation.3 | async-start | bytes 3760128 | tf_op jit(solution)/shard_map/reduce_scatter | solution.py:88
  272.3 9.0 %collective-permute-start.23 = (bf16[4,1,48,256]{3,2,1,0:T(8,128)(2,1)S(1)}, bf16[4,1,48,256]{3,2,1,0:T(8,128)(2,1)S(1)}, u32[]{:S(2)}, u32[]{:S(2)}) collective-permute-start(bf16[4,1,48,256]{3,2,1,0:T(8,128)(2,1)S(1)} %get-tuple-element.33), channel_id=1, source_target_pairs={{1,0},{2,1},{3,2},{4,3},{5,4},{6,5},{7,6},{8,7},{9,8},{10,9},{11,1... | collective-permute-start | bytes 294920 | tf_op jit(solution)/shard_map/ppermute | solution.py:30
  311.1 251.3 %all-reduce.6.cloned.1.call-start = ((), (), s32[]{:S(2)}) async-start(), calls=%async_computation.5 | async-start | bytes 884736 | tf_op jit(solution)/shard_map/psum | solution.py:91
  (11 other events, 76.7 us)
Sparse Core Ops, SparseCore 0:
  12.8 75.3 all-gather.1
  270.9 132.0 reduce-scatter.4
  408.1 134.3 reduce-scatter.2
  544.8 17.5 all-reduce.5
